TPU v7x, 512 devices: a whole 4x4x16 slice. The times are simulated.
512 devices in a mesh: blk: 16 (over z), pen: 32 (over x, y, core).
Axes of the slice: x: 4, y: 4, z: 16, core: 2. Of those that a mesh axis runs over, the one named last changes fastest.
Arguments:
- state: bfloat16 [16, 2, 32, 512, 512], P('blk', None, None, 'pen'), may hold values from -6 to 6
- inverse_x: bfloat16 [16, 2, 512, 512], P('blk')
- inverse_y: bfloat16 [16, 2, 512, 512], P('blk')
- rates: float32 [16, 3], P('blk'), may hold values from 0.05 to 0.4
- partner: int32 [16, 2], P('blk'), may hold values from 0 to 15
- face_side: int32 [16, 2], P('blk'), may hold values from 0 to 1
- orient: int32 [16, 2], P('blk'), may hold values from 0 to 1
- offset: int32 [16, 2], P('blk'), may hold values from 0 to 31
Outputs:
- relaxed: bfloat16 [16, 2, 32, 512, 512], P('blk', None, None, 'pen')
All inputs are finite; a program needn't handle non-finite values.
Results may differ from a plain program's by a relative error of at most 0.0058.
Values may be sent and summed in bfloat16 or wider, within the bound.
No kernel may reach another device: no remote copies, remote signals or barrier semaphores. Data moves between devices by JAX's collectives and lax.ppermute only.
A program may use at most 64 MiB of HBM per device.

v0:
```python
import jax
import jax.numpy as jnp
from jax import lax
from jax.sharding import PartitionSpec as P

STEPS = 2


def plane_ghosts(layers, partner_row, side_row, orient_row, offset_row, tile_rows):
    blocks = lax.all_gather(layers[None], "blk", axis=0, tiled=True)
    lines = layers.shape[-1]
    rows_y = jnp.arange(lines, dtype=jnp.int32)
    result = []
    for which in range(2):
        piece = lax.dynamic_index_in_dim(blocks, partner_row[which], 0, keepdims=False)
        segment = lax.dynamic_index_in_dim(piece, side_row[which], 0, keepdims=False)
        mirrored = jnp.where(orient_row[which] == 1, lines - 1 - rows_y, rows_y)
        take_at = (mirrored + offset_row[which] * tile_rows) % lines
        result.append(jnp.take(segment, take_at, axis=-1))
    return result


def local(state, inverse_x, inverse_y, rates, partner, face_side, orient, offset):
    magnet = state[0]
    inv_x = inverse_x[0]
    inv_y = inverse_y[0]
    rate_row = rates[0]
    first_col = inv_x[:, :, 0].astype(jnp.float32)
    last_col = inv_x[:, :, -1].astype(jnp.float32)
    tile_rows = magnet.shape[2]
    planes = lax.all_to_all(magnet, "pen", split_axis=1, concat_axis=2, tiled=True)
    for repeat in range(STEPS):
        layers = jnp.stack([planes[..., 0], planes[..., -1]], axis=0)
        ghosts = plane_ghosts(layers, partner[0], face_side[0], orient[0], offset[0], tile_rows)
        interior = jnp.einsum("fax,fzyx->fzya", inv_x, planes, preferred_element_type=jnp.float32)
        edges = first_col[:, None, None, :] * ghosts[0].astype(jnp.float32)[..., None]
        edges = edges + last_col[:, None, None, :] * ghosts[1].astype(jnp.float32)[..., None]
        swept_x = (interior + edges).astype(jnp.bfloat16)
        swept_y = jnp.einsum("fcy,fzyx->fzcx", inv_y, swept_x, preferred_element_type=jnp.float32)
        proton = swept_y[0]
        carbon = swept_y[1]
        new_proton = proton - (rate_row[0] * proton + rate_row[2] * carbon)
        new_carbon = carbon - (rate_row[1] * carbon + rate_row[2] * proton)
        planes = jnp.stack([new_proton, new_carbon]).astype(jnp.bfloat16)
    magnet = lax.all_to_all(planes, "pen", split_axis=2, concat_axis=1, tiled=True)
    return magnet[None]


def solution(mesh):
    return jax.shard_map(
        local,
        mesh=mesh,
        in_specs=(
            P("blk", None, None, "pen", None),
            P("blk", None, None, None),
            P("blk", None, None, None),
            P("blk", None),
            P("blk", None),
            P("blk", None),
            P("blk", None),
            P("blk", None),
        ),
        out_specs=P("blk", None, None, "pen", None),
        check_vma=False,
    )
```

profile of v0, /device:TPU:1, one launch (start us, length us, event | category | flops | bytes accessed | tf_op | source)
XLA Modules:
  0.0 137.5 jit_solution(13616519110712983959)
XLA Ops:
  0.0 0.0 copy-start
  0.0 0.0 copy-start.9
  0.0 0.0 copy-start.10
  0.0 0.0 copy-start.3
  0.0 0.0 copy-start.1
  0.1 2.4 %copy.81 = bf16[1,2,32,16,512]{4,3,1,2,0:T(8,128)(2,1)} copy(bf16[1,2,32,16,512]{4,3,2,1,0:T(8,128)(2,1)} %param.10) | data formatting | bytes 2097152 | tf_op args[0]
  2.5 10.5 %all-to-all-start = ((bf16[2,32,16,512]{3,2,0,1:T(8,128)(2,1)}), bf16[2,32,16,512]{3,2,0,1:T(8,128)(2,1)S(1)}, u32[]{:S(2)}, u32[]{:S(2)}) async-start(bf16[2,32,16,512]{3,2,0,1:T(8,128)(2,1)} %bitcast.95), calls=%async_computation | async-start | bytes 2097152 | tf_op jit(solution)/shard_map/all_to_all | solution.py:31
  12.9 0.0 copy-done.7
  13.0 0.6 fusion.19
  16.1 0.0 copy-done.8
  16.1 0.6 fusion.18
  21.5 0.0 copy-done.9
  21.5 0.6 fusion.16
  23.4 0.0 copy-done.10
  23.4 0.7 fusion.17
  25.4 0.0 copy-start.5
  25.5 0.7 fusion.15
  26.2 0.3 convert_reduce_fusion.1
  26.5 3.5 %all-to-all-done = bf16[2,32,16,512]{3,2,0,1:T(8,128)(2,1)S(1)} async-done(((bf16[2,32,16,512]{3,2,0,1:T(8,128)(2,1)}), bf16[2,32,16,512]{3,2,0,1:T(8,128)(2,1)S(1)}, u32[]{:S(2)}, u32[]{:S(2)}) %all-to-all-start) | async-done | bytes 1048608 | tf_op jit(solution)/shard_map/all_to_all | solution.py:31
  29.9 0.1 copy.54
  30.0 0.3 slice_reduce_fusion.1
  30.4 26.5 %all-gather = bf16[32,2,1,512]{3,1,2,0:T(2,128)(2,1)S(1)} all-gather(bf16[2,2,1,512]{3,1,2,0:T(2,128)(2,1)S(1)} %pad_maximum_fusion.3), channel_id=2, replica_groups=mesh['blk'=16,'pen'=32] {'blk'}, dimensions={0}, use_global_device_ids=true | all-gather | bytes 69632 | tf_op jit(solution)/shard_map/all_gather | solution.py:10
  56.9 0.2 copy.74
  57.1 1.3 gather_fusion
  58.5 0.1 bitcast_convert_fusion.3
  58.6 0.1 copy.57
  58.7 0.2 copy.75
  58.9 1.3 gather_fusion.1
  60.3 0.1 bitcast_convert_fusion.2
  60.4 0.1 copy.59
  60.5 4.0 %convolution_bitcast_fusion.1 = f32[2,1,512,512]{2,3,0,1:T(8,128)} fusion(bf16[1,2,512,512]{3,2,1,0:T(8,128)(2,1)S(1)} %copy-done, bf16[2,512,512]{2,1,0:T(8,128)(2,1)S(1)} %bitcast.97, f32[2,512]{1,0:T(2,128)S(1)} %copy.59, f32[2,512]{1,0:T(2,128)S(1)} %get-tuple-element.7, f32[2,512]{1,0:T(2,128)S(1)} %copy.57, f32[2,512]{1,0:T(2,128)S(1)} %get-tuple-element.6, ...), kind=kOutput, calls=%fused_computation.7 | convolution fusion | flops 1076363264 | bytes 5259264 | tf_op jit(solution)/shard_map/fcy,fzyx->fzcx/dot_general | solution.py:39
  64.5 3.8 %subtract_convert_fusion.3 = (bf16[1,1,512,512]{2,3,0,1:T(8,128)(2,1)S(1)}, bf16[1,1,512,512]{2,3,0,1:T(8,128)(2,1)S(1)}) fusion(f32[2,1,512,512]{2,3,0,1:T(8,128)} %convolution_bitcast_fusion.1, f32[]{:T(128)} %bitcast.27, f32[]{:T(128)} %bitcast.26, f32[]{:T(128)} %bitcast.30), kind=kLoop, calls=%fused_computation.18 | loop fusion | flops 2621440 | bytes 3145740 | tf_op jit(solution)/shard_map/convert.13
  68.3 0.0 copy-start.2
  68.3 19.7 %all-gather.1 = bf16[32,2,1,512]{3,1,2,0:T(2,128)(2,1)S(1)} all-gather(bf16[2,2,1,512]{3,1,2,0:T(2,128)(2,1)S(1)} %pad_maximum_fusion.4), channel_id=3, replica_groups=mesh['blk'=16,'pen'=32] {'blk'}, dimensions={0}, use_global_device_ids=true | all-gather | bytes 69632 | tf_op jit(solution)/shard_map/all_gather | solution.py:10
  88.1 0.2 copy.76
  88.3 1.3 gather_fusion.2
  89.6 0.7 bitcast_convert_fusion.1
  90.4 0.1 copy.63
  90.5 0.2 copy.77
  90.7 1.3 gather_fusion.3
  92.0 0.7 bitcast_convert_fusion
  92.8 0.1 copy.65
  92.9 3.9 %convolution_bitcast_fusion = f32[2,1,512,512]{2,3,0,1:T(8,128)} fusion(bf16[1,2,512,512]{3,2,1,0:T(8,128)(2,1)S(1)} %copy-done, bf16[1,512,512]{1,2,0:T(8,128)(2,1)S(1)} %bitcast.99, bf16[1,512,512]{1,2,0:T(8,128)(2,1)S(1)} %bitcast.98, f32[2,512]{1,0:T(2,128)S(1)} %copy.65, f32[2,512]{1,0:T(2,128)S(1)} %copy.63, f32[2,512]{1,0:T(2,128)} %copy-done.4, ...), kind=kOutput, calls=%fused_computation.6 | convolution fusion | flops 1076887552 | bytes 5259264 | tf_op jit(solution)/shard_map/fcy,fzyx->fzcx/dot_general | solution.py:39
  96.8 3.8 %subtract_convert_fusion.1 = (bf16[1,1,512,512]{2,3,0,1:T(8,128)(2,1)S(1)}, bf16[1,1,512,512]{2,3,0,1:T(8,128)(2,1)S(1)}) fusion(f32[2,1,512,512]{2,3,0,1:T(8,128)} %convolution_bitcast_fusion, f32[]{:T(128)} %bitcast.27, f32[]{:T(128)} %bitcast.26, f32[]{:T(128)} %bitcast.30), kind=kLoop, calls=%fused_computation.16 | loop fusion | flops 2621440 | bytes 3145740 | tf_op jit(solution)/shard_map/convert.6
  100.6 0.1 pad_maximum_fusion
  100.7 1.0 copy.67
  101.7 34.6 %all_to_all.21 = bf16[2,1,512,512]{3,0,1,2:T(2,128)(2,1)S(1)} all-to-all(bf16[2,1,512,512]{3,0,1,2:T(2,128)(2,1)S(1)} %copy.67), channel_id=1, replica_groups=mesh['blk'=16,'pen'=32] {'pen'}, dimensions={2} | all-to-all | bytes 2097152 | tf_op jit(solution)/shard_map/all_to_all | solution.py:45
  136.3 1.1 copy.68
  (23 shorter events, 0.2 us)
Async XLA Ops:
  0.0 60.5 %copy-start = (bf16[1,2,512,512]{3,2,1,0:T(8,128)(2,1)S(1)}, bf16[1,2,512,512]{3,2,1,0:T(8,128)(2,1)}, u32[]{:S(2)}) copy-start(bf16[1,2,512,512]{3,2,1,0:T(8,128)(2,1)} %param.12) | copy-start | bytes 3145732
  0.0 12.9 %copy-start.7 = (s32[1,2]{1,0:T(1,128)S(1)}, s32[1,2]{1,0:T(1,128)}, u32[]{:S(2)}) copy-start(s32[1,2]{1,0:T(1,128)} %param.14) | copy-start | bytes 28
  0.0 16.1 %copy-start.8 = (s32[1,2]{1,0:T(1,128)S(1)}, s32[1,2]{1,0:T(1,128)}, u32[]{:S(2)}) copy-start(s32[1,2]{1,0:T(1,128)} %param.15) | copy-start | bytes 28
  0.0 21.5 %copy-start.9 = (s32[1,2]{1,0:T(1,128)S(1)}, s32[1,2]{1,0:T(1,128)}, u32[]{:S(2)}) copy-start(s32[1,2]{1,0:T(1,128)} %param.16) | copy-start | bytes 28
  0.0 23.3 %copy-start.10 = (s32[1,2]{1,0:T(1,128)S(1)}, s32[1,2]{1,0:T(1,128)}, u32[]{:S(2)}) copy-start(s32[1,2]{1,0:T(1,128)} %param.17) | copy-start | bytes 28
  0.0 25.5 %copy-start.3 = (f32[1,3]{1,0:T(1,128)S(1)}, f32[1,3]{1,0:T(1,128)}, u32[]{:S(2)}) copy-start(f32[1,3]{1,0:T(1,128)} %param.13) | copy-start | bytes 40
  0.0 26.1 %copy-start.1 = (bf16[1,2,512,512]{3,2,1,0:T(8,128)(2,1)S(1)}, bf16[1,2,512,512]{3,2,1,0:T(8,128)(2,1)}, u32[]{:S(2)}) copy-start(bf16[1,2,512,512]{3,2,1,0:T(8,128)(2,1)} %param.11) | copy-start | bytes 3145732
  2.5 27.5 %all-to-all-start = ((bf16[2,32,16,512]{3,2,0,1:T(8,128)(2,1)}), bf16[2,32,16,512]{3,2,0,1:T(8,128)(2,1)S(1)}, u32[]{:S(2)}, u32[]{:S(2)}) async-start(bf16[2,32,16,512]{3,2,0,1:T(8,128)(2,1)} %bitcast.95), calls=%async_computation | async-start | bytes 2097152 | tf_op jit(solution)/shard_map/all_to_all | solution.py:31
  25.4 33.5 %copy-start.6 = (pred[512]{0:T(512)(128)(4,1)}, pred[512]{0:T(512)(128)(4,1)S(1)}, u32[]{:S(2)}) copy-start(pred[512]{0:T(512)(128)(4,1)S(1)} %compare_and_fusion.1) | copy-start | bytes 1540
  25.4 34.8 %copy-start.5 = (pred[512]{0:T(512)(128)(4,1)}, pred[512]{0:T(512)(128)(4,1)S(1)}, u32[]{:S(2)}) copy-start(pred[512]{0:T(512)(128)(4,1)S(1)} %compare_and_fusion) | copy-start | bytes 1540
  26.5 34.0 %copy-start.4 = (f32[2,512]{1,0:T(2,128)}, f32[2,512]{1,0:T(2,128)S(1)}, u32[]{:S(2)}) copy-start(f32[2,512]{1,0:T(2,128)S(1)} %get-tuple-element.7) | copy-start | bytes 12292
  68.3 24.6 %copy-start.2 = (bf16[1,2,512,512]{3,2,1,0:T(8,128)(2,1)S(1)}, bf16[1,2,512,512]{3,2,1,0:T(8,128)(2,1)}, u32[]{:S(2)}) copy-start(bf16[1,2,512,512]{3,2,1,0:T(8,128)(2,1)} %param.11) | copy-start | bytes 3145732
where the time goes:
time: 138 us; the launch traced here: 137 us
  blocking collectives  80.9 us (59%)
  local copies, waits for them, and re-layouts  14.7 us (11%)
  starting transfers between devices  10.5 us (8%)
  between operations  10.2 us (7%)
  other arithmetic  9.87 us (7%)
  matrix products  7.85 us (6%)
  waiting for transfers between devices  3.45 us (2%)
    all_gather x2, blocking collectives, plane_ghosts(): blocks = lax.all_gather(layers[None], 'blk', axis=0, tiled=True)  46.3 us
    all_to_all x1, blocking collectives, local(): lax.all_to_all(planes, 'pen', split_axis=2, concat_axis=1, tiled=True)  34.6 us
    all_to_all x1, starting transfers between devices, local(): lax.all_to_all(magnet, 'pen', split_axis=1, concat_axis=2, tiled=True)  10.5 us
    dot_general x2, matrix products, local(): jnp.einsum('fcy,fzyx->fzcx', inv_y, swept_x, preferred_element_type=jnp.f...  7.85 us
    another operation x2, other arithmetic  7.59 us
    gather x4, local copies, waits for them, and re-layouts, plane_ghosts(): result.append(jnp.take(segment, take_at, axis=-1))  5.36 us
    all_to_all x1, waiting for transfers between devices, local(): lax.all_to_all(magnet, 'pen', split_axis=1, concat_axis=2, tiled=True)  3.45 us
    unnamed x28, local copies, waits for them, and re-layouts  3.23 us
  transfers between devices with their start and end apart: 1, of which 1 were waited for; matrix products, arithmetic and copies ran while one was open for 3% of the time, Pallas kernels for 0%

commit v1 on v0

--- a/solution.py
+++ b/solution.py
@@ -7,7 +7,12 @@
 
 
 def plane_ghosts(layers, partner_row, side_row, orient_row, offset_row, tile_rows):
-    blocks = lax.all_gather(layers[None], "blk", axis=0, tiled=True)
+    ring = [layers[None]]
+    for hop in range(15):
+        ring.append(lax.ppermute(ring[-1], "blk", [(dev, (dev + 1) % 16) for dev in range(16)]))
+    blocks = jnp.roll(
+        jnp.concatenate(ring[::-1], axis=0), (lax.axis_index("blk") + 1) * ring[0].shape[0], axis=0
+    )
     lines = layers.shape[-1]
     rows_y = jnp.arange(lines, dtype=jnp.int32)
     result = []

time: 138 us -> 287 us (2.08)
  waiting for transfers between devices: 3.45 us -> 104 us
  starting transfers between devices: 10.5 us -> 57.7 us
    ppermute x0 -> x30, waiting for transfers between devices: none -> 104 us  [plane_ghosts(): lax.ppermute(ring[-1], 'blk', [(dev, (dev + 1) % 16) for dev in range(16)])]
    ppermute x0 -> x30, starting transfers between devices: none -> 57.7 us  [plane_ghosts(): lax.ppermute(ring[-1], 'blk', [(dev, (dev + 1) % 16) for dev in range(16)])]
    all_gather x2 -> x0, blocking collectives: 46.3 us -> none  [plane_ghosts(): blocks = lax.all_gather(layers[None], 'blk', axis=0, tiled=True)]
    all_to_all x0 -> x1, blocking collectives: none -> 26.7 us  [local(): lax.all_to_all(magnet, 'pen', split_axis=1, concat_axis=2, tiled=True)]
    all_to_all x1, blocking collectives: 34.6 us -> 53.5 us  [local(): lax.all_to_all(planes, 'pen', split_axis=2, concat_axis=1, tiled=True)]
    all_to_all x1 -> x0, starting transfers between devices: 10.5 us -> none  [local(): lax.all_to_all(magnet, 'pen', split_axis=1, concat_axis=2, tiled=True)]
    all_to_all x1 -> x0, waiting for transfers between devices: 3.45 us -> none  [local(): lax.all_to_all(magnet, 'pen', split_axis=1, concat_axis=2, tiled=True)]
    another operation x4 -> x2, other arithmetic: 7.61 us -> 7.53 us
  transfers between devices with their start and end apart: 1 -> 30, of which waited for: 1 -> 29; matrix products, arithmetic and copies ran while one was open for 3% -> 2% of each run, Pallas kernels for 0% -> 0%
where the time goes in v1:
time: 287 us; the launch traced here: 285 us
  waiting for transfers between devices  104 us (36%)
  blocking collectives  80.1 us (28%)
  starting transfers between devices  57.7 us (20%)
  local copies, waits for them, and re-layouts  14.6 us (5%)
  other arithmetic  11 us (4%)
  between operations  10.5 us (4%)
  matrix products  7.27 us (3%)
    ppermute x30, waiting for transfers between devices, plane_ghosts(): lax.ppermute(ring[-1], 'blk', [(dev, (dev + 1) % 16) for dev in range(16)])  104 us
    ppermute x30, starting transfers between devices, plane_ghosts(): lax.ppermute(ring[-1], 'blk', [(dev, (dev + 1) % 16) for dev in range(16)])  57.7 us
    all_to_all x1, blocking collectives, local(): lax.all_to_all(planes, 'pen', split_axis=2, concat_axis=1, tiled=True)  53.5 us
    all_to_all x1, blocking collectives, local(): lax.all_to_all(magnet, 'pen', split_axis=1, concat_axis=2, tiled=True)  26.7 us
    another operation x2, other arithmetic  7.53 us
    dot_general x2, matrix products, local(): jnp.einsum('fcy,fzyx->fzcx', inv_y, swept_x, preferred_element_type=jnp.f...  7.27 us
  transfers between devices with their start and end apart: 30, of which 29 were waited for; matrix products, arithmetic and copies ran while one was open for 2% of the time, Pallas kernels for 0%

profile of v1, /device:TPU:1, one launch (start us, length us, event | category | flops | bytes accessed | tf_op | source)
XLA Modules:
  0.0 285.3 jit_solution(652110809813496359)
XLA Ops:
  1.4 26.7 %all_to_all.21 = bf16[2,32,16,512]{3,2,0,1:T(8,128)(2,1)S(1)} all-to-all(bf16[2,32,16,512]{3,2,0,1:T(8,128)(2,1)S(1)} %bitcast.102), channel_id=1, replica_groups=mesh['blk'=16,'pen'=32] {'pen'}, dimensions={1} | all-to-all | bytes 2097152 | tf_op jit(solution)/shard_map/all_to_all | solution.py:36
  28.5 2.3 collective-permute-start
  30.8 8.6 %collective-permute-done = bf16[1,2,2,1,512]{4,2,1,3,0:T(2,128)(2,1)S(1)} collective-permute-done((bf16[1,2,2,1,512]{4,2,1,3,0:T(2,128)(2,1)S(1)}, bf16[1,2,2,1,512]{4,2,1,3,0:T(2,128)(2,1)S(1)}, u32[]{:S(2)}, u32[]{:S(2)}) %collective-permute-start) | collective-permute-done | bytes 4128 | tf_op jit(solution)/shard_map/ppermute | solution.py:12
  39.4 1.9 collective-permute-start.1
  41.3 3.6 %collective-permute-done.1 = bf16[1,2,2,1,512]{4,2,1,3,0:T(2,128)(2,1)S(1)} collective-permute-done((bf16[1,2,2,1,512]{4,2,1,3,0:T(2,128)(2,1)S(1)}, bf16[1,2,2,1,512]{4,2,1,3,0:T(2,128)(2,1)S(1)}, u32[]{:S(2)}, u32[]{:S(2)}) %collective-permute-start.1) | collective-permute-done | bytes 4128 | tf_op jit(solution)/shard_map/ppermute | solution.py:12
  45.0 1.9 collective-permute-start.2
  46.9 3.6 %collective-permute-done.2 = bf16[1,2,2,1,512]{4,2,1,3,0:T(2,128)(2,1)S(1)} collective-permute-done((bf16[1,2,2,1,512]{4,2,1,3,0:T(2,128)(2,1)S(1)}, bf16[1,2,2,1,512]{4,2,1,3,0:T(2,128)(2,1)S(1)}, u32[]{:S(2)}, u32[]{:S(2)}) %collective-permute-start.2) | collective-permute-done | bytes 4128 | tf_op jit(solution)/shard_map/ppermute | solution.py:12
  50.5 1.9 collective-permute-start.3
  52.4 3.6 %collective-permute-done.3 = bf16[1,2,2,1,512]{4,2,1,3,0:T(2,128)(2,1)S(1)} collective-permute-done((bf16[1,2,2,1,512]{4,2,1,3,0:T(2,128)(2,1)S(1)}, bf16[1,2,2,1,512]{4,2,1,3,0:T(2,128)(2,1)S(1)}, u32[]{:S(2)}, u32[]{:S(2)}) %collective-permute-start.3) | collective-permute-done | bytes 4128 | tf_op jit(solution)/shard_map/ppermute | solution.py:12
  56.1 1.9 collective-permute-start.4
  58.0 3.6 %collective-permute-done.4 = bf16[1,2,2,1,512]{4,2,1,3,0:T(2,128)(2,1)S(1)} collective-permute-done((bf16[1,2,2,1,512]{4,2,1,3,0:T(2,128)(2,1)S(1)}, bf16[1,2,2,1,512]{4,2,1,3,0:T(2,128)(2,1)S(1)}, u32[]{:S(2)}, u32[]{:S(2)}) %collective-permute-start.4) | collective-permute-done | bytes 4128 | tf_op jit(solution)/shard_map/ppermute | solution.py:12
  64.4 2.7 collective-permute-done.5
  69.7 3.0 %collective-permute-done.6 = bf16[1,2,2,1,512]{4,2,1,3,0:T(2,128)(2,1)S(1)} collective-permute-done((bf16[1,2,2,1,512]{4,2,1,3,0:T(2,128)(2,1)S(1)}, bf16[1,2,2,1,512]{4,2,1,3,0:T(2,128)(2,1)S(1)}, u32[]{:S(2)}, u32[]{:S(2)}) %collective-permute-start.6) | collective-permute-done | bytes 4128 | tf_op jit(solution)/shard_map/ppermute | solution.py:12
  72.7 1.9 collective-permute-start.7
  75.2 3.0 %collective-permute-done.7 = bf16[1,2,2,1,512]{4,2,1,3,0:T(2,128)(2,1)S(1)} collective-permute-done((bf16[1,2,2,1,512]{4,2,1,3,0:T(2,128)(2,1)S(1)}, bf16[1,2,2,1,512]{4,2,1,3,0:T(2,128)(2,1)S(1)}, u32[]{:S(2)}, u32[]{:S(2)}) %collective-permute-start.7) | collective-permute-done | bytes 4128 | tf_op jit(solution)/shard_map/ppermute | solution.py:12
  80.8 3.0 %collective-permute-done.8 = bf16[1,2,2,1,512]{4,2,1,3,0:T(2,128)(2,1)S(1)} collective-permute-done((bf16[1,2,2,1,512]{4,2,1,3,0:T(2,128)(2,1)S(1)}, bf16[1,2,2,1,512]{4,2,1,3,0:T(2,128)(2,1)S(1)}, u32[]{:S(2)}, u32[]{:S(2)}) %collective-permute-start.8) | collective-permute-done | bytes 4128 | tf_op jit(solution)/shard_map/ppermute | solution.py:12
  86.3 3.0 %collective-permute-done.9 = bf16[1,2,2,1,512]{4,2,1,3,0:T(2,128)(2,1)S(1)} collective-permute-done((bf16[1,2,2,1,512]{4,2,1,3,0:T(2,128)(2,1)S(1)}, bf16[1,2,2,1,512]{4,2,1,3,0:T(2,128)(2,1)S(1)}, u32[]{:S(2)}, u32[]{:S(2)}) %collective-permute-start.9) | collective-permute-done | bytes 4128 | tf_op jit(solution)/shard_map/ppermute | solution.py:12
  89.4 1.9 collective-permute-start.10
  96.9 3.6 %collective-permute-done.11 = bf16[1,2,2,1,512]{4,2,1,3,0:T(2,128)(2,1)S(1)} collective-permute-done((bf16[1,2,2,1,512]{4,2,1,3,0:T(2,128)(2,1)S(1)}, bf16[1,2,2,1,512]{4,2,1,3,0:T(2,128)(2,1)S(1)}, u32[]{:S(2)}, u32[]{:S(2)}) %collective-permute-start.11) | collective-permute-done | bytes 4128 | tf_op jit(solution)/shard_map/ppermute | solution.py:12
  100.5 1.9 collective-permute-start.12
  102.4 3.6 %collective-permute-done.12 = bf16[1,2,2,1,512]{4,2,1,3,0:T(2,128)(2,1)S(1)} collective-permute-done((bf16[1,2,2,1,512]{4,2,1,3,0:T(2,128)(2,1)S(1)}, bf16[1,2,2,1,512]{4,2,1,3,0:T(2,128)(2,1)S(1)}, u32[]{:S(2)}, u32[]{:S(2)}) %collective-permute-start.12) | collective-permute-done | bytes 4128 | tf_op jit(solution)/shard_map/ppermute | solution.py:12
  107.9 3.6 %collective-permute-done.13 = bf16[1,2,2,1,512]{4,2,1,3,0:T(2,128)(2,1)S(1)} collective-permute-done((bf16[1,2,2,1,512]{4,2,1,3,0:T(2,128)(2,1)S(1)}, bf16[1,2,2,1,512]{4,2,1,3,0:T(2,128)(2,1)S(1)}, u32[]{:S(2)}, u32[]{:S(2)}) %collective-permute-start.13) | collective-permute-done | bytes 4128 | tf_op jit(solution)/shard_map/ppermute | solution.py:12
  126.7 3.4 %convolution_bitcast_fusion.1 = f32[2,1,512,512]{2,3,0,1:T(8,128)} fusion(bf16[1,2,512,512]{3,2,1,0:T(8,128)(2,1)S(1)} %copy-done, bf16[2,512,512]{2,1,0:T(8,128)(2,1)S(1)} %bitcast.104, f32[2,512]{1,0:T(2,128)S(1)} %copy.123, f32[2,512]{1,0:T(2,128)} %get-tuple-element.8, f32[2,512]{1,0:T(2,128)} %copy.121, f32[2,512]{1,0:T(2,128)} %get-tuple-element.6, ...), kind=kOutput, calls=%fused_computation.7 | convolution fusion | flops 1076363264 | bytes 5259264 | tf_op jit(solution)/shard_map/fcy,fzyx->fzcx/dot_general | solution.py:44
  130.1 3.8 %subtract_convert_fusion.3 = (bf16[1,1,512,512]{2,3,0,1:T(8,128)(2,1)S(1)}, bf16[1,1,512,512]{2,3,0,1:T(8,128)(2,1)S(1)}) fusion(f32[2,1,512,512]{2,3,0,1:T(8,128)} %convolution_bitcast_fusion.1, f32[]{:T(128)} %bitcast.27, f32[]{:T(128)} %bitcast.26, f32[]{:T(128)} %bitcast.30), kind=kLoop, calls=%fused_computation.18 | loop fusion | flops 2621440 | bytes 3145740 | tf_op jit(solution)/shard_map/convert.13
  133.9 1.9 collective-permute-start.15
  135.8 3.6 %collective-permute-done.15 = bf16[1,2,2,1,512]{4,2,1,3,0:T(2,128)(2,1)S(1)} collective-permute-done((bf16[1,2,2,1,512]{4,2,1,3,0:T(2,128)(2,1)S(1)}, bf16[1,2,2,1,512]{4,2,1,3,0:T(2,128)(2,1)S(1)}, u32[]{:S(2)}, u32[]{:S(2)}) %collective-permute-start.15) | collective-permute-done | bytes 4128 | tf_op jit(solution)/shard_map/ppermute | solution.py:12
  139.5 1.9 collective-permute-start.16
  141.4 3.6 %collective-permute-done.16 = bf16[1,2,2,1,512]{4,2,1,3,0:T(2,128)(2,1)S(1)} collective-permute-done((bf16[1,2,2,1,512]{4,2,1,3,0:T(2,128)(2,1)S(1)}, bf16[1,2,2,1,512]{4,2,1,3,0:T(2,128)(2,1)S(1)}, u32[]{:S(2)}, u32[]{:S(2)}) %collective-permute-start.16) | collective-permute-done | bytes 4128 | tf_op jit(solution)/shard_map/ppermute | solution.py:12
  147.0 3.6 %collective-permute-done.17 = bf16[1,2,2,1,512]{4,2,1,3,0:T(2,128)(2,1)S(1)} collective-permute-done((bf16[1,2,2,1,512]{4,2,1,3,0:T(2,128)(2,1)S(1)}, bf16[1,2,2,1,512]{4,2,1,3,0:T(2,128)(2,1)S(1)}, u32[]{:S(2)}, u32[]{:S(2)}) %collective-permute-start.17) | collective-permute-done | bytes 4128 | tf_op jit(solution)/shard_map/ppermute | solution.py:12
  152.5 3.7 %collective-permute-done.18 = bf16[1,2,2,1,512]{4,2,1,3,0:T(2,128)(2,1)S(1)} collective-permute-done((bf16[1,2,2,1,512]{4,2,1,3,0:T(2,128)(2,1)S(1)}, bf16[1,2,2,1,512]{4,2,1,3,0:T(2,128)(2,1)S(1)}, u32[]{:S(2)}, u32[]{:S(2)}) %collective-permute-start.18) | collective-permute-done | bytes 4128 | tf_op jit(solution)/shard_map/ppermute | solution.py:12
  158.1 3.6 %collective-permute-done.19 = bf16[1,2,2,1,512]{4,2,1,3,0:T(2,128)(2,1)S(1)} collective-permute-done((bf16[1,2,2,1,512]{4,2,1,3,0:T(2,128)(2,1)S(1)}, bf16[1,2,2,1,512]{4,2,1,3,0:T(2,128)(2,1)S(1)}, u32[]{:S(2)}, u32[]{:S(2)}) %collective-permute-start.19) | collective-permute-done | bytes 4128 | tf_op jit(solution)/shard_map/ppermute | solution.py:12
  161.7 1.9 collective-permute-start.20
  163.7 3.6 %collective-permute-done.20 = bf16[1,2,2,1,512]{4,2,1,3,0:T(2,128)(2,1)S(1)} collective-permute-done((bf16[1,2,2,1,512]{4,2,1,3,0:T(2,128)(2,1)S(1)}, bf16[1,2,2,1,512]{4,2,1,3,0:T(2,128)(2,1)S(1)}, u32[]{:S(2)}, u32[]{:S(2)}) %collective-permute-start.20) | collective-permute-done | bytes 4128 | tf_op jit(solution)/shard_map/ppermute | solution.py:12
  169.2 3.6 %collective-permute-done.21 = bf16[1,2,2,1,512]{4,2,1,3,0:T(2,128)(2,1)S(1)} collective-permute-done((bf16[1,2,2,1,512]{4,2,1,3,0:T(2,128)(2,1)S(1)}, bf16[1,2,2,1,512]{4,2,1,3,0:T(2,128)(2,1)S(1)}, u32[]{:S(2)}, u32[]{:S(2)}) %collective-permute-start.21) | collective-permute-done | bytes 4128 | tf_op jit(solution)/shard_map/ppermute | solution.py:12
  174.8 3.6 %collective-permute-done.22 = bf16[1,2,2,1,512]{4,2,1,3,0:T(2,128)(2,1)S(1)} collective-permute-done((bf16[1,2,2,1,512]{4,2,1,3,0:T(2,128)(2,1)S(1)}, bf16[1,2,2,1,512]{4,2,1,3,0:T(2,128)(2,1)S(1)}, u32[]{:S(2)}, u32[]{:S(2)}) %collective-permute-start.22) | collective-permute-done | bytes 4128 | tf_op jit(solution)/shard_map/ppermute | solution.py:12
  178.4 1.9 collective-permute-start.23
  180.3 3.6 %collective-permute-done.23 = bf16[1,2,2,1,512]{4,2,1,3,0:T(2,128)(2,1)S(1)} collective-permute-done((bf16[1,2,2,1,512]{4,2,1,3,0:T(2,128)(2,1)S(1)}, bf16[1,2,2,1,512]{4,2,1,3,0:T(2,128)(2,1)S(1)}, u32[]{:S(2)}, u32[]{:S(2)}) %collective-permute-start.23) | collective-permute-done | bytes 4128 | tf_op jit(solution)/shard_map/ppermute | solution.py:12
  185.9 3.8 %collective-permute-done.24 = bf16[1,2,2,1,512]{4,2,1,3,0:T(2,128)(2,1)S(1)} collective-permute-done((bf16[1,2,2,1,512]{4,2,1,3,0:T(2,128)(2,1)S(1)}, bf16[1,2,2,1,512]{4,2,1,3,0:T(2,128)(2,1)S(1)}, u32[]{:S(2)}, u32[]{:S(2)}) %collective-permute-start.24) | collective-permute-done | bytes 4128 | tf_op jit(solution)/shard_map/ppermute | solution.py:12
  189.7 1.9 collective-permute-start.25
  191.6 3.6 %collective-permute-done.25 = bf16[1,2,2,1,512]{4,2,1,3,0:T(2,128)(2,1)S(1)} collective-permute-done((bf16[1,2,2,1,512]{4,2,1,3,0:T(2,128)(2,1)S(1)}, bf16[1,2,2,1,512]{4,2,1,3,0:T(2,128)(2,1)S(1)}, u32[]{:S(2)}, u32[]{:S(2)}) %collective-permute-start.25) | collective-permute-done | bytes 4128 | tf_op jit(solution)/shard_map/ppermute | solution.py:12
  197.2 3.6 %collective-permute-done.26 = bf16[1,2,2,1,512]{4,2,1,3,0:T(2,128)(2,1)S(1)} collective-permute-done((bf16[1,2,2,1,512]{4,2,1,3,0:T(2,128)(2,1)S(1)}, bf16[1,2,2,1,512]{4,2,1,3,0:T(2,128)(2,1)S(1)}, u32[]{:S(2)}, u32[]{:S(2)}) %collective-permute-start.26) | collective-permute-done | bytes 4128 | tf_op jit(solution)/shard_map/ppermute | solution.py:12
  202.7 3.6 %collective-permute-done.27 = bf16[1,2,2,1,512]{4,2,1,3,0:T(2,128)(2,1)S(1)} collective-permute-done((bf16[1,2,2,1,512]{4,2,1,3,0:T(2,128)(2,1)S(1)}, bf16[1,2,2,1,512]{4,2,1,3,0:T(2,128)(2,1)S(1)}, u32[]{:S(2)}, u32[]{:S(2)}) %collective-permute-start.27) | collective-permute-done | bytes 4128 | tf_op jit(solution)/shard_map/ppermute | solution.py:12
  206.4 1.9 collective-permute-start.28
  208.3 3.6 %collective-permute-done.28 = bf16[1,2,2,1,512]{4,2,1,3,0:T(2,128)(2,1)S(1)} collective-permute-done((bf16[1,2,2,1,512]{4,2,1,3,0:T(2,128)(2,1)S(1)}, bf16[1,2,2,1,512]{4,2,1,3,0:T(2,128)(2,1)S(1)}, u32[]{:S(2)}, u32[]{:S(2)}) %collective-permute-start.28) | collective-permute-done | bytes 4128 | tf_op jit(solution)/shard_map/ppermute | solution.py:12
  213.8 3.6 %collective-permute-done.29 = bf16[1,2,2,1,512]{4,2,1,3,0:T(2,128)(2,1)S(1)} collective-permute-done((bf16[1,2,2,1,512]{4,2,1,3,0:T(2,128)(2,1)S(1)}, bf16[1,2,2,1,512]{4,2,1,3,0:T(2,128)(2,1)S(1)}, u32[]{:S(2)}, u32[]{:S(2)}) %collective-permute-start.29) | collective-permute-done | bytes 4128 | tf_op jit(solution)/shard_map/ppermute | solution.py:12
  221.9 3.9 %convolution_bitcast_fusion = f32[2,1,512,512]{2,3,0,1:T(8,128)} fusion(bf16[1,2,512,512]{3,2,1,0:T(8,128)(2,1)S(1)} %copy-done, bf16[1,512,512]{1,2,0:T(8,128)(2,1)S(1)} %bitcast.106, bf16[1,512,512]{1,2,0:T(8,128)(2,1)S(1)} %bitcast.105, f32[2,512]{1,0:T(2,128)S(1)} %copy.129, f32[2,512]{1,0:T(2,128)S(1)} %copy.127, f32[2,512]{1,0:T(2,128)} %get-tuple-element.8, ...), kind=kOutput, calls=%fused_computation.6 | convolution fusion | flops 1076887552 | bytes 5259264 | tf_op jit(solution)/shard_map/fcy,fzyx->fzcx/dot_general | solution.py:44
  225.8 3.8 %subtract_convert_fusion.1 = (bf16[1,1,512,512]{2,3,0,1:T(8,128)(2,1)S(1)}, bf16[1,1,512,512]{2,3,0,1:T(8,128)(2,1)S(1)}) fusion(f32[2,1,512,512]{2,3,0,1:T(8,128)} %convolution_bitcast_fusion, f32[]{:T(128)} %bitcast.27, f32[]{:T(128)} %bitcast.26, f32[]{:T(128)} %bitcast.30), kind=kLoop, calls=%fused_computation.16 | loop fusion | flops 2621440 | bytes 3145740 | tf_op jit(solution)/shard_map/convert.6
  230.7 53.5 %all_to_all.22 = bf16[2,1,512,512]{3,0,1,2:T(2,128)(2,1)S(1)} all-to-all(bf16[2,1,512,512]{3,0,1,2:T(2,128)(2,1)S(1)} %copy.131), channel_id=1, replica_groups=mesh['blk'=16,'pen'=32] {'pen'}, dimensions={2} | all-to-all | bytes 2097152 | tf_op jit(solution)/shard_map/all_to_all | solution.py:50
  (104 shorter events, 49.1 us)
Async XLA Ops:
  0.0 126.7 %copy-start = (bf16[1,2,512,512]{3,2,1,0:T(8,128)(2,1)S(1)}, bf16[1,2,512,512]{3,2,1,0:T(8,128)(2,1)}, u32[]{:S(2)}) copy-start(bf16[1,2,512,512]{3,2,1,0:T(8,128)(2,1)} %param.14) | copy-start | bytes 3145732
  1.4 62.1 %copy-start.1 = (bf16[1,2,512,512]{3,2,1,0:T(8,128)(2,1)S(1)}, bf16[1,2,512,512]{3,2,1,0:T(8,128)(2,1)}, u32[]{:S(2)}) copy-start(bf16[1,2,512,512]{3,2,1,0:T(8,128)(2,1)} %param.13) | copy-start | bytes 3145732
  28.1 41.0 %copy-start.2 = (f32[1,3]{1,0:T(1,128)S(1)}, f32[1,3]{1,0:T(1,128)}, u32[]{:S(2)}) copy-start(f32[1,3]{1,0:T(1,128)} %param.15) | copy-start | bytes 40
  28.1 46.5 %copy-start.3 = (s32[1,2]{1,0:T(1,128)S(1)}, s32[1,2]{1,0:T(1,128)}, u32[]{:S(2)}) copy-start(s32[1,2]{1,0:T(1,128)} %param.16) | copy-start | bytes 28
  28.1 52.1 %copy-start.4 = (s32[1,2]{1,0:T(1,128)S(1)}, s32[1,2]{1,0:T(1,128)}, u32[]{:S(2)}) copy-start(s32[1,2]{1,0:T(1,128)} %param.17) | copy-start | bytes 28
  28.1 57.6 %copy-start.5 = (s32[1,2]{1,0:T(1,128)S(1)}, s32[1,2]{1,0:T(1,128)}, u32[]{:S(2)}) copy-start(s32[1,2]{1,0:T(1,128)} %param.18) | copy-start | bytes 28
  28.1 63.2 %copy-start.6 = (s32[1,2]{1,0:T(1,128)S(1)}, s32[1,2]{1,0:T(1,128)}, u32[]{:S(2)}) copy-start(s32[1,2]{1,0:T(1,128)} %param.19) | copy-start | bytes 28
  28.5 10.9 %collective-permute-start = (bf16[1,2,2,1,512]{4,2,1,3,0:T(2,128)(2,1)S(1)}, bf16[1,2,2,1,512]{4,2,1,3,0:T(2,128)(2,1)S(1)}, u32[]{:S(2)}, u32[]{:S(2)}) collective-permute-start(bf16[1,2,2,1,512]{4,2,1,3,0:T(2,128)(2,1)S(1)} %maximum_bitcast_fusion), channel_id=1, source_target_pairs={{0,32},{32,64},{64,96},{96,128},{128,160},{160,192},{192,224},{224... | collective-permute-start | bytes 12296 | tf_op jit(solution)/shard_map/ppermute | solution.py:12
  39.4 5.6 %collective-permute-start.1 = (bf16[1,2,2,1,512]{4,2,1,3,0:T(2,128)(2,1)S(1)}, bf16[1,2,2,1,512]{4,2,1,3,0:T(2,128)(2,1)S(1)}, u32[]{:S(2)}, u32[]{:S(2)}) collective-permute-start(bf16[1,2,2,1,512]{4,2,1,3,0:T(2,128)(2,1)S(1)} %collective-permute-done), channel_id=1, source_target_pairs={{0,32},{32,64},{64,96},{96,128},{128,160},{160,192},{192,224},{224... | collective-permute-start | bytes 12296 | tf_op jit(solution)/shard_map/ppermute | solution.py:12
  45.0 5.6 %collective-permute-start.2 = (bf16[1,2,2,1,512]{4,2,1,3,0:T(2,128)(2,1)S(1)}, bf16[1,2,2,1,512]{4,2,1,3,0:T(2,128)(2,1)S(1)}, u32[]{:S(2)}, u32[]{:S(2)}) collective-permute-start(bf16[1,2,2,1,512]{4,2,1,3,0:T(2,128)(2,1)S(1)} %collective-permute-done.1), channel_id=1, source_target_pairs={{0,32},{32,64},{64,96},{96,128},{128,160},{160,192},{192,224},{224... | collective-permute-start | bytes 12296 | tf_op jit(solution)/shard_map/ppermute | solution.py:12
  50.5 5.6 %collective-permute-start.3 = (bf16[1,2,2,1,512]{4,2,1,3,0:T(2,128)(2,1)S(1)}, bf16[1,2,2,1,512]{4,2,1,3,0:T(2,128)(2,1)S(1)}, u32[]{:S(2)}, u32[]{:S(2)}) collective-permute-start(bf16[1,2,2,1,512]{4,2,1,3,0:T(2,128)(2,1)S(1)} %collective-permute-done.2), channel_id=1, source_target_pairs={{0,32},{32,64},{64,96},{96,128},{128,160},{160,192},{192,224},{224... | collective-permute-start | bytes 12296 | tf_op jit(solution)/shard_map/ppermute | solution.py:12
  56.1 5.6 %collective-permute-start.4 = (bf16[1,2,2,1,512]{4,2,1,3,0:T(2,128)(2,1)S(1)}, bf16[1,2,2,1,512]{4,2,1,3,0:T(2,128)(2,1)S(1)}, u32[]{:S(2)}, u32[]{:S(2)}) collective-permute-start(bf16[1,2,2,1,512]{4,2,1,3,0:T(2,128)(2,1)S(1)} %collective-permute-done.3), channel_id=1, source_target_pairs={{0,32},{32,64},{64,96},{96,128},{128,160},{160,192},{192,224},{224... | collective-permute-start | bytes 12296 | tf_op jit(solution)/shard_map/ppermute | solution.py:12
  61.6 5.6 %collective-permute-start.5 = (bf16[1,2,2,1,512]{4,2,1,3,0:T(2,128)(2,1)S(1)}, bf16[1,2,2,1,512]{4,2,1,3,0:T(2,128)(2,1)S(1)}, u32[]{:S(2)}, u32[]{:S(2)}) collective-permute-start(bf16[1,2,2,1,512]{4,2,1,3,0:T(2,128)(2,1)S(1)} %collective-permute-done.4), channel_id=1, source_target_pairs={{0,32},{32,64},{64,96},{96,128},{128,160},{160,192},{192,224},{224... | collective-permute-start | bytes 12296 | tf_op jit(solution)/shard_map/ppermute | solution.py:12
  67.2 5.6 %collective-permute-start.6 = (bf16[1,2,2,1,512]{4,2,1,3,0:T(2,128)(2,1)S(1)}, bf16[1,2,2,1,512]{4,2,1,3,0:T(2,128)(2,1)S(1)}, u32[]{:S(2)}, u32[]{:S(2)}) collective-permute-start(bf16[1,2,2,1,512]{4,2,1,3,0:T(2,128)(2,1)S(1)} %collective-permute-done.5), channel_id=1, source_target_pairs={{0,32},{32,64},{64,96},{96,128},{128,160},{160,192},{192,224},{224... | collective-permute-start | bytes 12296 | tf_op jit(solution)/shard_map/ppermute | solution.py:12
  72.7 5.6 %collective-permute-start.7 = (bf16[1,2,2,1,512]{4,2,1,3,0:T(2,128)(2,1)S(1)}, bf16[1,2,2,1,512]{4,2,1,3,0:T(2,128)(2,1)S(1)}, u32[]{:S(2)}, u32[]{:S(2)}) collective-permute-start(bf16[1,2,2,1,512]{4,2,1,3,0:T(2,128)(2,1)S(1)} %collective-permute-done.6), channel_id=1, source_target_pairs={{0,32},{32,64},{64,96},{96,128},{128,160},{160,192},{192,224},{224... | collective-permute-start | bytes 12296 | tf_op jit(solution)/shard_map/ppermute | solution.py:12
  78.3 5.6 %collective-permute-start.8 = (bf16[1,2,2,1,512]{4,2,1,3,0:T(2,128)(2,1)S(1)}, bf16[1,2,2,1,512]{4,2,1,3,0:T(2,128)(2,1)S(1)}, u32[]{:S(2)}, u32[]{:S(2)}) collective-permute-start(bf16[1,2,2,1,512]{4,2,1,3,0:T(2,128)(2,1)S(1)} %collective-permute-done.7), channel_id=1, source_target_pairs={{0,32},{32,64},{64,96},{96,128},{128,160},{160,192},{192,224},{224... | collective-permute-start | bytes 12296 | tf_op jit(solution)/shard_map/ppermute | solution.py:12
  83.8 5.6 %collective-permute-start.9 = (bf16[1,2,2,1,512]{4,2,1,3,0:T(2,128)(2,1)S(1)}, bf16[1,2,2,1,512]{4,2,1,3,0:T(2,128)(2,1)S(1)}, u32[]{:S(2)}, u32[]{:S(2)}) collective-permute-start(bf16[1,2,2,1,512]{4,2,1,3,0:T(2,128)(2,1)S(1)} %collective-permute-done.8), channel_id=1, source_target_pairs={{0,32},{32,64},{64,96},{96,128},{128,160},{160,192},{192,224},{224... | collective-permute-start | bytes 12296 | tf_op jit(solution)/shard_map/ppermute | solution.py:12
  89.4 5.6 %collective-permute-start.10 = (bf16[1,2,2,1,512]{4,2,1,3,0:T(2,128)(2,1)S(1)}, bf16[1,2,2,1,512]{4,2,1,3,0:T(2,128)(2,1)S(1)}, u32[]{:S(2)}, u32[]{:S(2)}) collective-permute-start(bf16[1,2,2,1,512]{4,2,1,3,0:T(2,128)(2,1)S(1)} %collective-permute-done.9), channel_id=1, source_target_pairs={{0,32},{32,64},{64,96},{96,128},{128,160},{160,192},{192,224},{224... | collective-permute-start | bytes 12296 | tf_op jit(solution)/shard_map/ppermute | solution.py:12
  94.9 5.6 %collective-permute-start.11 = (bf16[1,2,2,1,512]{4,2,1,3,0:T(2,128)(2,1)S(1)}, bf16[1,2,2,1,512]{4,2,1,3,0:T(2,128)(2,1)S(1)}, u32[]{:S(2)}, u32[]{:S(2)}) collective-permute-start(bf16[1,2,2,1,512]{4,2,1,3,0:T(2,128)(2,1)S(1)} %collective-permute-done.10), channel_id=1, source_target_pairs={{0,32},{32,64},{64,96},{96,128},{128,160},{160,192},{192,224},{224... | collective-permute-start | bytes 12296 | tf_op jit(solution)/shard_map/ppermute | solution.py:12
  100.5 5.6 %collective-permute-start.12 = (bf16[1,2,2,1,512]{4,2,1,3,0:T(2,128)(2,1)S(1)}, bf16[1,2,2,1,512]{4,2,1,3,0:T(2,128)(2,1)S(1)}, u32[]{:S(2)}, u32[]{:S(2)}) collective-permute-start(bf16[1,2,2,1,512]{4,2,1,3,0:T(2,128)(2,1)S(1)} %collective-permute-done.11), channel_id=1, source_target_pairs={{0,32},{32,64},{64,96},{96,128},{128,160},{160,192},{192,224},{224... | collective-permute-start | bytes 12296 | tf_op jit(solution)/shard_map/ppermute | solution.py:12
  106.0 5.6 %collective-permute-start.13 = (bf16[1,2,2,1,512]{4,2,1,3,0:T(2,128)(2,1)S(1)}, bf16[1,2,2,1,512]{4,2,1,3,0:T(2,128)(2,1)S(1)}, u32[]{:S(2)}, u32[]{:S(2)}) collective-permute-start(bf16[1,2,2,1,512]{4,2,1,3,0:T(2,128)(2,1)S(1)} %collective-permute-done.12), channel_id=1, source_target_pairs={{0,32},{32,64},{64,96},{96,128},{128,160},{160,192},{192,224},{224... | collective-permute-start | bytes 12296 | tf_op jit(solution)/shard_map/ppermute | solution.py:12
  111.6 10.1 %collective-permute-start.14 = (bf16[1,2,2,1,512]{4,2,1,3,0:T(2,128)(2,1)S(1)}, bf16[1,2,2,1,512]{4,2,1,3,0:T(2,128)(2,1)S(1)}, u32[]{:S(2)}, u32[]{:S(2)}) collective-permute-start(bf16[1,2,2,1,512]{4,2,1,3,0:T(2,128)(2,1)S(1)} %collective-permute-done.13), channel_id=1, source_target_pairs={{0,32},{32,64},{64,96},{96,128},{128,160},{160,192},{192,224},{224... | collective-permute-start | bytes 12296 | tf_op jit(solution)/shard_map/ppermute | solution.py:12
  133.9 5.6 %collective-permute-start.15 = (bf16[1,2,2,1,512]{4,2,1,3,0:T(2,128)(2,1)S(1)}, bf16[1,2,2,1,512]{4,2,1,3,0:T(2,128)(2,1)S(1)}, u32[]{:S(2)}, u32[]{:S(2)}) collective-permute-start(bf16[1,2,2,1,512]{4,2,1,3,0:T(2,128)(2,1)S(1)} %maximum_bitcast_fusion.1), channel_id=1, source_target_pairs={{0,32},{32,64},{64,96},{96,128},{128,160},{160,192},{192,224},{224... | collective-permute-start | bytes 12296 | tf_op jit(solution)/shard_map/ppermute | solution.py:12
  139.5 5.6 %collective-permute-start.16 = (bf16[1,2,2,1,512]{4,2,1,3,0:T(2,128)(2,1)S(1)}, bf16[1,2,2,1,512]{4,2,1,3,0:T(2,128)(2,1)S(1)}, u32[]{:S(2)}, u32[]{:S(2)}) collective-permute-start(bf16[1,2,2,1,512]{4,2,1,3,0:T(2,128)(2,1)S(1)} %collective-permute-done.15), channel_id=1, source_target_pairs={{0,32},{32,64},{64,96},{96,128},{128,160},{160,192},{192,224},{224... | collective-permute-start | bytes 12296 | tf_op jit(solution)/shard_map/ppermute | solution.py:12
  145.0 5.6 %collective-permute-start.17 = (bf16[1,2,2,1,512]{4,2,1,3,0:T(2,128)(2,1)S(1)}, bf16[1,2,2,1,512]{4,2,1,3,0:T(2,128)(2,1)S(1)}, u32[]{:S(2)}, u32[]{:S(2)}) collective-permute-start(bf16[1,2,2,1,512]{4,2,1,3,0:T(2,128)(2,1)S(1)} %collective-permute-done.16), channel_id=1, source_target_pairs={{0,32},{32,64},{64,96},{96,128},{128,160},{160,192},{192,224},{224... | collective-permute-start | bytes 12296 | tf_op jit(solution)/shard_map/ppermute | solution.py:12
  150.6 5.6 %collective-permute-start.18 = (bf16[1,2,2,1,512]{4,2,1,3,0:T(2,128)(2,1)S(1)}, bf16[1,2,2,1,512]{4,2,1,3,0:T(2,128)(2,1)S(1)}, u32[]{:S(2)}, u32[]{:S(2)}) collective-permute-start(bf16[1,2,2,1,512]{4,2,1,3,0:T(2,128)(2,1)S(1)} %collective-permute-done.17), channel_id=1, source_target_pairs={{0,32},{32,64},{64,96},{96,128},{128,160},{160,192},{192,224},{224... | collective-permute-start | bytes 12296 | tf_op jit(solution)/shard_map/ppermute | solution.py:12
  156.2 5.6 %collective-permute-start.19 = (bf16[1,2,2,1,512]{4,2,1,3,0:T(2,128)(2,1)S(1)}, bf16[1,2,2,1,512]{4,2,1,3,0:T(2,128)(2,1)S(1)}, u32[]{:S(2)}, u32[]{:S(2)}) collective-permute-start(bf16[1,2,2,1,512]{4,2,1,3,0:T(2,128)(2,1)S(1)} %collective-permute-done.18), channel_id=1, source_target_pairs={{0,32},{32,64},{64,96},{96,128},{128,160},{160,192},{192,224},{224... | collective-permute-start | bytes 12296 | tf_op jit(solution)/shard_map/ppermute | solution.py:12
  161.7 5.6 %collective-permute-start.20 = (bf16[1,2,2,1,512]{4,2,1,3,0:T(2,128)(2,1)S(1)}, bf16[1,2,2,1,512]{4,2,1,3,0:T(2,128)(2,1)S(1)}, u32[]{:S(2)}, u32[]{:S(2)}) collective-permute-start(bf16[1,2,2,1,512]{4,2,1,3,0:T(2,128)(2,1)S(1)} %collective-permute-done.19), channel_id=1, source_target_pairs={{0,32},{32,64},{64,96},{96,128},{128,160},{160,192},{192,224},{224... | collective-permute-start | bytes 12296 | tf_op jit(solution)/shard_map/ppermute | solution.py:12
  167.3 5.6 %collective-permute-start.21 = (bf16[1,2,2,1,512]{4,2,1,3,0:T(2,128)(2,1)S(1)}, bf16[1,2,2,1,512]{4,2,1,3,0:T(2,128)(2,1)S(1)}, u32[]{:S(2)}, u32[]{:S(2)}) collective-permute-start(bf16[1,2,2,1,512]{4,2,1,3,0:T(2,128)(2,1)S(1)} %collective-permute-done.20), channel_id=1, source_target_pairs={{0,32},{32,64},{64,96},{96,128},{128,160},{160,192},{192,224},{224... | collective-permute-start | bytes 12296 | tf_op jit(solution)/shard_map/ppermute | solution.py:12
  172.8 5.6 %collective-permute-start.22 = (bf16[1,2,2,1,512]{4,2,1,3,0:T(2,128)(2,1)S(1)}, bf16[1,2,2,1,512]{4,2,1,3,0:T(2,128)(2,1)S(1)}, u32[]{:S(2)}, u32[]{:S(2)}) collective-permute-start(bf16[1,2,2,1,512]{4,2,1,3,0:T(2,128)(2,1)S(1)} %collective-permute-done.21), channel_id=1, source_target_pairs={{0,32},{32,64},{64,96},{96,128},{128,160},{160,192},{192,224},{224... | collective-permute-start | bytes 12296 | tf_op jit(solution)/shard_map/ppermute | solution.py:12
  178.4 5.6 %collective-permute-start.23 = (bf16[1,2,2,1,512]{4,2,1,3,0:T(2,128)(2,1)S(1)}, bf16[1,2,2,1,512]{4,2,1,3,0:T(2,128)(2,1)S(1)}, u32[]{:S(2)}, u32[]{:S(2)}) collective-permute-start(bf16[1,2,2,1,512]{4,2,1,3,0:T(2,128)(2,1)S(1)} %collective-permute-done.22), channel_id=1, source_target_pairs={{0,32},{32,64},{64,96},{96,128},{128,160},{160,192},{192,224},{224... | collective-permute-start | bytes 12296 | tf_op jit(solution)/shard_map/ppermute | solution.py:12
  184.0 5.7 %collective-permute-start.24 = (bf16[1,2,2,1,512]{4,2,1,3,0:T(2,128)(2,1)S(1)}, bf16[1,2,2,1,512]{4,2,1,3,0:T(2,128)(2,1)S(1)}, u32[]{:S(2)}, u32[]{:S(2)}) collective-permute-start(bf16[1,2,2,1,512]{4,2,1,3,0:T(2,128)(2,1)S(1)} %collective-permute-done.23), channel_id=1, source_target_pairs={{0,32},{32,64},{64,96},{96,128},{128,160},{160,192},{192,224},{224... | collective-permute-start | bytes 12296 | tf_op jit(solution)/shard_map/ppermute | solution.py:12
  189.7 5.6 %collective-permute-start.25 = (bf16[1,2,2,1,512]{4,2,1,3,0:T(2,128)(2,1)S(1)}, bf16[1,2,2,1,512]{4,2,1,3,0:T(2,128)(2,1)S(1)}, u32[]{:S(2)}, u32[]{:S(2)}) collective-permute-start(bf16[1,2,2,1,512]{4,2,1,3,0:T(2,128)(2,1)S(1)} %collective-permute-done.24), channel_id=1, source_target_pairs={{0,32},{32,64},{64,96},{96,128},{128,160},{160,192},{192,224},{224... | collective-permute-start | bytes 12296 | tf_op jit(solution)/shard_map/ppermute | solution.py:12
  195.2 5.6 %collective-permute-start.26 = (bf16[1,2,2,1,512]{4,2,1,3,0:T(2,128)(2,1)S(1)}, bf16[1,2,2,1,512]{4,2,1,3,0:T(2,128)(2,1)S(1)}, u32[]{:S(2)}, u32[]{:S(2)}) collective-permute-start(bf16[1,2,2,1,512]{4,2,1,3,0:T(2,128)(2,1)S(1)} %collective-permute-done.25), channel_id=1, source_target_pairs={{0,32},{32,64},{64,96},{96,128},{128,160},{160,192},{192,224},{224... | collective-permute-start | bytes 12296 | tf_op jit(solution)/shard_map/ppermute | solution.py:12
  200.8 5.6 %collective-permute-start.27 = (bf16[1,2,2,1,512]{4,2,1,3,0:T(2,128)(2,1)S(1)}, bf16[1,2,2,1,512]{4,2,1,3,0:T(2,128)(2,1)S(1)}, u32[]{:S(2)}, u32[]{:S(2)}) collective-permute-start(bf16[1,2,2,1,512]{4,2,1,3,0:T(2,128)(2,1)S(1)} %collective-permute-done.26), channel_id=1, source_target_pairs={{0,32},{32,64},{64,96},{96,128},{128,160},{160,192},{192,224},{224... | collective-permute-start | bytes 12296 | tf_op jit(solution)/shard_map/ppermute | solution.py:12
  206.4 5.6 %collective-permute-start.28 = (bf16[1,2,2,1,512]{4,2,1,3,0:T(2,128)(2,1)S(1)}, bf16[1,2,2,1,512]{4,2,1,3,0:T(2,128)(2,1)S(1)}, u32[]{:S(2)}, u32[]{:S(2)}) collective-permute-start(bf16[1,2,2,1,512]{4,2,1,3,0:T(2,128)(2,1)S(1)} %collective-permute-done.27), channel_id=1, source_target_pairs={{0,32},{32,64},{64,96},{96,128},{128,160},{160,192},{192,224},{224... | collective-permute-start | bytes 12296 | tf_op jit(solution)/shard_map/ppermute | solution.py:12
  211.9 5.6 %collective-permute-start.29 = (bf16[1,2,2,1,512]{4,2,1,3,0:T(2,128)(2,1)S(1)}, bf16[1,2,2,1,512]{4,2,1,3,0:T(2,128)(2,1)S(1)}, u32[]{:S(2)}, u32[]{:S(2)}) collective-permute-start(bf16[1,2,2,1,512]{4,2,1,3,0:T(2,128)(2,1)S(1)} %collective-permute-done.28), channel_id=1, source_target_pairs={{0,32},{32,64},{64,96},{96,128},{128,160},{160,192},{192,224},{224... | collective-permute-start | bytes 12296 | tf_op jit(solution)/shard_map/ppermute | solution.py:12
